TPU v7x, 512 devices: a whole 4x8x8 slice. The times are simulated.
512 devices in a mesh: edp: 16 (over z, core), ep: 32 (over y, x).
Axes of the slice: x: 4, y: 8, z: 8, core: 2. Of those that a mesh axis runs over, the one named last changes fastest.
Arguments:
- token_acts: bfloat16 [16, 32, 2, 64, 1024], P('edp', 'ep'), may hold values from -6 to 6
- out_grad: bfloat16 [16, 32, 3584, 128], P('edp', 'ep'), may hold values from -0.59765625 to 0.59765625
- counts: int32 [16, 32, 2], P('edp', 'ep'), may hold values from 1 to 64, as said below
- params: float32 [32, 3584, 1024], P('ep', 'edp'), may hold values from -3 to 3
- first_moment: bfloat16 [32, 3584, 1024], P('ep', 'edp'), may hold values from -3 to 3
- second_moment: bfloat16 [32, 3584, 1024], P('ep', 'edp'), may hold values from 0.049804688 to 2
- old_expert: int32 [32], replicated, may hold values from 0 to 31, each once
- replica_of: int32 [32], replicated, may hold values from 0 to 31
- new_expert: int32 [32], replicated, may hold values from 0 to 31, each once
Outputs:
- update_step: float32 [32, 3584, 1024], P('ep', 'edp')
- new_first: bfloat16 [32, 3584, 1024], P('ep', 'edp')
- new_second: bfloat16 [32, 3584, 1024], P('ep', 'edp')
Inputs may be any that keep to these rules, and one draw needn't show every extreme that they name: `counts`: every slot has at least one live token; some slot is full and some slot has exactly one live token in every draw. `old_expert`: each expert appears exactly once. `new_expert`: each expert appears exactly once. `replica_of`: any expert may be served by any number of replica slots, its owner's included.
All inputs are finite; a program needn't handle non-finite values.
Results may differ from a plain program's by a relative error of at most 0.015.
Values may be sent and summed in bfloat16 or wider, within the bound.
A program may use at most 64 MiB of HBM per device.

v0:
```python
import jax
import jax.numpy as jnp
from jax import lax
from jax.sharding import PartitionSpec as P

beta_one = 0.9
beta_two = 0.95
bias_one = 0.9999734386011124
bias_two = 0.994079470779666
decay_rate = 0.1
adam_eps = 1e-08


def adam_update(weights, first_old, second_old, gradient):
    first_new = beta_one * first_old.astype(jnp.float32) + (1.0 - beta_one) * gradient
    second_new = beta_two * second_old.astype(jnp.float32) + (1.0 - beta_two) * gradient * gradient
    scaled = first_new / bias_one / (jnp.sqrt(second_new / bias_two) + adam_eps)
    step_new = -(scaled + decay_rate * weights)
    return (step_new, first_new.astype(jnp.bfloat16), second_new.astype(jnp.bfloat16))


def local(
    token_acts,
    out_grad,
    counts,
    params,
    first_moment,
    second_moment,
    old_expert,
    replica_of,
    new_expert,
):
    groups = lax.axis_size("edp")
    owners = lax.axis_size("ep")
    model_width = out_grad.shape[2]
    slot_count = token_acts.shape[2]
    tok_slot = token_acts.shape[3]
    hidden_units = token_acts.shape[4]
    row_count = model_width // groups
    piece_len = row_count * hidden_units // owners
    local_grad = out_grad[0, 0]
    local_counts = counts[0, 0]
    column = jnp.arange(slot_count * tok_slot, dtype=jnp.int32)
    slot_index = column // tok_slot
    live_limit = jnp.where(slot_index == 0, local_counts[0], local_counts[1])
    live_mask = column % tok_slot < live_limit
    masked = jnp.where(live_mask[None, :], local_grad, jnp.zeros_like(local_grad))
    received = lax.all_to_all(
        masked.reshape(groups, row_count, slot_count * tok_slot),
        "edp",
        split_axis=0,
        concat_axis=0,
        tiled=True,
    )
    arrived = lax.all_gather(token_acts[0], "edp", axis=0, tiled=True)
    count_here = arrived.shape[0]
    grad_block = received
    grad_block = grad_block.reshape(count_here, row_count, slot_count, tok_slot)
    slot_grads = jnp.einsum(
        "adst,astf->sdf", grad_block, arrived, preferred_element_type=jnp.float32
    )
    own_grad = slot_grads[0].reshape(owners, piece_len)
    replica_grad = slot_grads[1].reshape(owners, piece_len)
    sum_matrix = (replica_of[None, :] == old_expert[:, None]).astype(jnp.float32)
    move_matrix = (old_expert[None, :] == new_expert[:, None]).astype(jnp.float32)
    weights = params[0].reshape(owners, piece_len)
    first_old = first_moment[0].reshape(owners, piece_len)
    second_old = second_moment[0].reshape(owners, piece_len)
    replica_sent = lax.all_to_all(
        replica_grad.astype(jnp.bfloat16), "ep", split_axis=0, concat_axis=0, tiled=True
    ).astype(replica_grad.dtype)
    set_sums = jnp.dot(sum_matrix, replica_sent, precision=lax.Precision.HIGHEST)
    returned = lax.all_to_all(
        set_sums.astype(jnp.bfloat16), "ep", split_axis=0, concat_axis=0, tiled=True
    ).astype(set_sums.dtype)
    weights, first_old, second_old = adam_update(
        weights, first_old, second_old, own_grad + returned
    )
    weight_pieces = lax.all_to_all(weights, "ep", split_axis=0, concat_axis=0, tiled=True)
    first_pieces, second_pieces = (
        lax.all_to_all(first_old, "ep", split_axis=0, concat_axis=0, tiled=True),
        lax.all_to_all(second_old, "ep", split_axis=0, concat_axis=0, tiled=True),
    )
    placed_steps = jnp.dot(move_matrix, weight_pieces, precision=lax.Precision.HIGHEST)
    move_half = move_matrix.astype(jnp.bfloat16)
    placed_first = jnp.dot(move_half, first_pieces, preferred_element_type=jnp.float32).astype(
        jnp.bfloat16
    )
    placed_second = jnp.dot(move_half, second_pieces, preferred_element_type=jnp.float32).astype(
        jnp.bfloat16
    )
    final_steps = lax.all_to_all(placed_steps, "ep", split_axis=0, concat_axis=0, tiled=True)
    final_first, final_second = (
        lax.all_to_all(placed_first, "ep", split_axis=0, concat_axis=0, tiled=True),
        lax.all_to_all(placed_second, "ep", split_axis=0, concat_axis=0, tiled=True),
    )
    return (
        final_steps.reshape(1, row_count, hidden_units),
        final_first.reshape(1, row_count, hidden_units),
        final_second.reshape(1, row_count, hidden_units),
    )


def solution(mesh):
    return jax.shard_map(
        local,
        mesh=mesh,
        in_specs=(
            P("edp", "ep", None, None, None),
            P("edp", "ep", None, None),
            P("edp", "ep", None),
            P("ep", "edp", None),
            P("ep", "edp", None),
            P("ep", "edp", None),
            P(),
            P(),
            P(),
        ),
        out_specs=(P("ep", "edp", None), P("ep", "edp", None), P("ep", "edp", None)),
        check_vma=False,
    )
```

profile of v0, /device:TPU:2, one launch (start us, length us, event | category | flops | bytes accessed | tf_op | source)
XLA Modules:
  0.0 280.3 jit_solution(12393630941862970195)
XLA Ops:
  7.2 0.7 all-gather.3.cloned.1.call-update
  7.9 1.3 fusion.33
  9.2 1.3 fusion.30
  10.5 1.2 broadcast_select_fusion
  11.8 41.0 %all_to_all.77 = bf16[16,224,128]{2,1,0:T(8,128)(2,1)S(1)} all-to-all(bf16[16,224,128]{2,1,0:T(8,128)(2,1)S(1)} %broadcast_select_fusion), channel_id=1, replica_groups=mesh['edp'=16,'ep'=32] {'edp'}, dimensions={0} | all-to-all | bytes 1835008 | tf_op jit(solution)/shard_map/all_to_all | solution.py:48
  52.7 0.5 copy.31
  53.3 18.0 %all-gather.3.cloned.1.call-done = bf16[16,1,2,64,1024]{4,3,2,1,0:T(8,128)(2,1)} async-done(((bf16[1,1,2,64,1024]{4,3,2,1,0:T(8,128)(2,1)}), bf16[16,1,2,64,1024]{4,3,2,1,0:T(8,128)(2,1)}) %all-gather.3.cloned.1.call-update) | async-done | bytes 4194320 | tf_op jit(solution)/shard_map/all_gather | solution.py:55
  71.3 3.3 %fusion.5 = f32[2,224,1024]{2,1,0:T(8,128)S(1)} fusion(bf16[16,224,2,64]{1,3,2,0:T(8,128)(2,1)S(1)} %bitcast.32, bf16[16,1,2,64,1024]{4,3,2,1,0:T(8,128)(2,1)} %all-gather.3.cloned.1.call-done), kind=kOutput, calls=%fused_computation.9 | convolution fusion | flops 939524096 | bytes 6946816 | tf_op jit(solution)/shard_map/adst,astf->sdf/dot_general | solution.py:59
  74.7 0.1 slice.22
  74.8 0.4 convert_element_type.77
  75.1 0.5 broadcast.125
  75.7 3.3 %reduce.3 = bf16[32,7168]{1,0:T(8,128)(2,1)S(1)} reduce(bf16[32,1,7168]{2,1,0:T(2,128)(2,1)S(1)} %convert_element_type.77, bf16[]{:T(256)} %broadcast.125), dimensions={1}, to_apply=%convert_element_type.77.reduce_sub_computation | reduce | bytes 917506 | tf_op jit(solution)/shard_map/convert_element_type | solution.py:70
  79.0 0.3 reshape.144
  79.3 25.9 %all_to_all.78 = bf16[32,2,3584]{2,1,0:T(2,128)(2,1)S(1)} all-to-all(bf16[32,2,3584]{2,1,0:T(2,128)(2,1)S(1)} %reshape.144), channel_id=1, replica_groups=mesh['edp'=16,'ep'=32] {'ep'}, dimensions={0} | all-to-all | bytes 917504 | tf_op jit(solution)/shard_map/all_to_all | solution.py:69
  105.2 0.4 reshape.145
  105.6 0.3 fusion.2
  105.9 0.8 reduce.4
  106.8 1.1 reshape.146
  107.8 5.6 %all-to-all-start.2 = ((bf16[32,2,3584]{2,1,0:T(2,128)(2,1)}), bf16[32,2,3584]{2,1,0:T(2,128)(2,1)S(1)}, u32[]{:S(2)}, u32[]{:S(2)}) async-start(bf16[32,2,3584]{2,1,0:T(2,128)(2,1)} %reshape.146), calls=%async_computation.2 | async-start | bytes 917504 | tf_op jit(solution)/shard_map/all_to_all | solution.py:73
  113.4 2.2 broadcast_multiply_fusion
  115.7 1.6 mul.76
  117.2 2.1 convert_multiply_fusion.1
  119.3 2.6 mul.67
  121.9 2.0 convert_multiply_fusion
  123.9 2.5 mul.71
  126.4 1.0 slice.19
  127.4 1.6 reshape_squeeze.2
  129.0 1.1 reshape.147
  130.2 3.1 %fusion.32 = (bf16[32,1,7168]{2,0,1:T(8,128)(2,1)}, f32[32,1,7168]{2,0,1:T(8,128)S(1)}, bf16[32,1,7168]{2,0,1:T(8,128)(2,1)S(1)}) fusion(f32[32,1,7168]{2,0,1:T(8,128)} %mul.71, f32[32,1,7168]{2,0,1:T(8,128)S(1)} %reshape_squeeze.2, bf16[32,1,7168]{2,1,0:T(2,128)(2,1)} %reshape.147, f32[32,1,7168]{2,0,1:T(8,128)S(1)} %mul.76, f32[32,1,7168]{2,0,1:T(8,128)} %mul.67), kind=kLoop, calls=%fused_computation.47 | loop fusion | flops 3440640 | bytes 5963776 | tf_op jit(solution)/shard_map/convert_element_type | solution.py:19
  133.3 1.9 reduce.7
  135.2 1.1 reshape.152
  136.3 9.8 %all-to-all-start.7 = ((bf16[32,2,3584]{2,1,0:T(2,128)(2,1)}), bf16[32,2,3584]{2,1,0:T(2,128)(2,1)S(1)}, u32[]{:S(2)}, u32[]{:S(2)}) async-start(bf16[32,2,3584]{2,1,0:T(2,128)(2,1)} %reshape.152), calls=%async_computation.7 | async-start | bytes 917504 | tf_op jit(solution)/shard_map/all_to_all | solution.py:82
  146.1 0.8 reduce.5
  146.9 1.1 reshape.148
  148.0 12.1 %all-to-all-done.7 = bf16[32,2,3584]{2,1,0:T(2,128)(2,1)S(1)} async-done(((bf16[32,2,3584]{2,1,0:T(2,128)(2,1)}), bf16[32,2,3584]{2,1,0:T(2,128)(2,1)S(1)}, u32[]{:S(2)}, u32[]{:S(2)}) %all-to-all-start.7) | async-done | bytes 458784 | tf_op jit(solution)/shard_map/all_to_all | solution.py:82
  160.1 5.7 %all-to-all-start.5 = ((bf16[32,2,3584]{2,1,0:T(2,128)(2,1)}), bf16[32,2,3584]{2,1,0:T(2,128)(2,1)S(1)}, u32[]{:S(2)}, u32[]{:S(2)}) async-start(bf16[32,2,3584]{2,1,0:T(2,128)(2,1)} %reshape.148), calls=%async_computation.5 | async-start | bytes 917504 | tf_op jit(solution)/shard_map/all_to_all | solution.py:81
  165.9 0.4 reshape.153
  166.3 0.3 fusion.1
  166.6 0.8 reduce.8
  167.5 1.1 reshape.154
  168.6 10.7 %all-to-all-done.5 = bf16[32,2,3584]{2,1,0:T(2,128)(2,1)S(1)} async-done(((bf16[32,2,3584]{2,1,0:T(2,128)(2,1)}), bf16[32,2,3584]{2,1,0:T(2,128)(2,1)S(1)}, u32[]{:S(2)}, u32[]{:S(2)}) %all-to-all-start.5) | async-done | bytes 458784 | tf_op jit(solution)/shard_map/all_to_all | solution.py:81
  179.3 5.6 %all-to-all-start.8 = ((bf16[32,2,3584]{2,1,0:T(2,128)(2,1)}), bf16[32,2,3584]{2,1,0:T(2,128)(2,1)S(1)}, u32[]{:S(2)}, u32[]{:S(2)}) async-start(bf16[32,2,3584]{2,1,0:T(2,128)(2,1)} %reshape.154), calls=%async_computation.8 | async-start | bytes 917504 | tf_op jit(solution)/shard_map/all_to_all | solution.py:95
  184.9 1.9 copy.35
  186.7 11.1 %all-to-all-done.8 = bf16[32,2,3584]{2,1,0:T(2,128)(2,1)S(1)} async-done(((bf16[32,2,3584]{2,1,0:T(2,128)(2,1)}), bf16[32,2,3584]{2,1,0:T(2,128)(2,1)S(1)}, u32[]{:S(2)}, u32[]{:S(2)}) %all-to-all-start.8) | async-done | bytes 458784 | tf_op jit(solution)/shard_map/all_to_all | solution.py:95
  197.9 5.6 %all-to-all-start.3 = ((f32[32,1,7168]{2,1,0:T(1,128)}), f32[32,1,7168]{2,1,0:T(1,128)S(1)}, u32[]{:S(2)}, u32[]{:S(2)}) async-start(f32[32,1,7168]{2,1,0:T(1,128)} %copy.35), calls=%async_computation.3 | async-start | bytes 1835008 | tf_op jit(solution)/shard_map/all_to_all | solution.py:79
  203.4 0.4 reshape.149
  203.8 0.3 fusion
  204.2 0.8 reduce.6
  205.0 1.1 reshape.150
  206.1 19.8 %all-to-all-done.3 = f32[32,1,7168]{2,1,0:T(1,128)S(1)} async-done(((f32[32,1,7168]{2,1,0:T(1,128)}), f32[32,1,7168]{2,1,0:T(1,128)S(1)}, u32[]{:S(2)}, u32[]{:S(2)}) %all-to-all-start.3) | async-done | bytes 917536 | tf_op jit(solution)/shard_map/all_to_all | solution.py:79
  225.9 5.6 %all-to-all-start.6 = ((bf16[32,2,3584]{2,1,0:T(2,128)(2,1)}), bf16[32,2,3584]{2,1,0:T(2,128)(2,1)S(1)}, u32[]{:S(2)}, u32[]{:S(2)}) async-start(bf16[32,2,3584]{2,1,0:T(2,128)(2,1)} %reshape.150), calls=%async_computation.6 | async-start | bytes 917504 | tf_op jit(solution)/shard_map/all_to_all | solution.py:94
  231.5 0.6 convolution_bitcast_fusion
  232.1 1.9 copy.36
  234.0 9.8 %all-to-all-done.6 = bf16[32,2,3584]{2,1,0:T(2,128)(2,1)S(1)} async-done(((bf16[32,2,3584]{2,1,0:T(2,128)(2,1)}), bf16[32,2,3584]{2,1,0:T(2,128)(2,1)S(1)}, u32[]{:S(2)}, u32[]{:S(2)}) %all-to-all-start.6) | async-done | bytes 458784 | tf_op jit(solution)/shard_map/all_to_all | solution.py:94
  243.7 5.6 %all-to-all-start.4 = ((f32[32,1,7168]{2,1,0:T(1,128)}), f32[32,1,7168]{2,1,0:T(1,128)S(1)}, u32[]{:S(2)}, u32[]{:S(2)}) async-start(f32[32,1,7168]{2,1,0:T(1,128)} %copy.36), calls=%async_computation.4 | async-start | bytes 1835008 | tf_op jit(solution)/shard_map/all_to_all | solution.py:92
  249.3 0.4 reshape.155
  249.7 2.7 reduce.2
  252.4 1.3 reshape.138
  253.7 0.4 reshape.151
  254.1 2.7 reduce.1
  256.8 1.3 reshape.137
  258.1 12.1 %all-to-all-done.4 = f32[32,1,7168]{2,1,0:T(1,128)S(1)} async-done(((f32[32,1,7168]{2,1,0:T(1,128)}), f32[32,1,7168]{2,1,0:T(1,128)S(1)}, u32[]{:S(2)}, u32[]{:S(2)}) %all-to-all-start.4) | async-done | bytes 917536 | tf_op jit(solution)/shard_map/all_to_all | solution.py:92
  270.2 2.2 reduce
  272.4 1.1 reshape.136
  (8 shorter events, 0.1 us)
Async XLA Ops:
  7.2 64.1 %all-gather.3.cloned.1.call-start = ((), (), s32[]{:S(2)}) async-start(), calls=%async_computation.9 | async-start | bytes 4456448 | tf_op jit(solution)/shard_map/all_gather | solution.py:55
  74.7 30.9 %copy-start = (s32[32]{0:T(128)S(1)}, s32[32]{0:T(128)}, u32[]{:S(2)}) copy-start(s32[32]{0:T(128)} %param.15) | copy-start | bytes 388
  74.7 30.9 %copy-start.2 = (s32[32]{0:T(128)S(1)}, s32[32]{0:T(128)}, u32[]{:S(2)}) copy-start(s32[32]{0:T(128)} %param.16) | copy-start | bytes 388
  107.8 21.2 %all-to-all-start.2 = ((bf16[32,2,3584]{2,1,0:T(2,128)(2,1)}), bf16[32,2,3584]{2,1,0:T(2,128)(2,1)S(1)}, u32[]{:S(2)}, u32[]{:S(2)}) async-start(bf16[32,2,3584]{2,1,0:T(2,128)(2,1)} %reshape.146), calls=%async_computation.2 | async-start | bytes 917504 | tf_op jit(solution)/shard_map/all_to_all | solution.py:73
  133.3 33.0 %copy-start.1 = (s32[32]{0:T(128)S(1)}, s32[32]{0:T(128)}, u32[]{:S(2)}) copy-start(s32[32]{0:T(128)} %param.17) | copy-start | bytes 388
  136.3 23.9 %all-to-all-start.7 = ((bf16[32,2,3584]{2,1,0:T(2,128)(2,1)}), bf16[32,2,3584]{2,1,0:T(2,128)(2,1)S(1)}, u32[]{:S(2)}, u32[]{:S(2)}) async-start(bf16[32,2,3584]{2,1,0:T(2,128)(2,1)} %reshape.152), calls=%async_computation.7 | async-start | bytes 917504 | tf_op jit(solution)/shard_map/all_to_all | solution.py:82
  160.1 19.2 %all-to-all-start.5 = ((bf16[32,2,3584]{2,1,0:T(2,128)(2,1)}), bf16[32,2,3584]{2,1,0:T(2,128)(2,1)S(1)}, u32[]{:S(2)}, u32[]{:S(2)}) async-start(bf16[32,2,3584]{2,1,0:T(2,128)(2,1)} %reshape.148), calls=%async_computation.5 | async-start | bytes 917504 | tf_op jit(solution)/shard_map/all_to_all | solution.py:81
  179.3 18.6 %all-to-all-start.8 = ((bf16[32,2,3584]{2,1,0:T(2,128)(2,1)}), bf16[32,2,3584]{2,1,0:T(2,128)(2,1)S(1)}, u32[]{:S(2)}, u32[]{:S(2)}) async-start(bf16[32,2,3584]{2,1,0:T(2,128)(2,1)} %reshape.154), calls=%async_computation.8 | async-start | bytes 917504 | tf_op jit(solution)/shard_map/all_to_all | solution.py:95
  197.9 28.0 %all-to-all-start.3 = ((f32[32,1,7168]{2,1,0:T(1,128)}), f32[32,1,7168]{2,1,0:T(1,128)S(1)}, u32[]{:S(2)}, u32[]{:S(2)}) async-start(f32[32,1,7168]{2,1,0:T(1,128)} %copy.35), calls=%async_computation.3 | async-start | bytes 1835008 | tf_op jit(solution)/shard_map/all_to_all | solution.py:79
  225.9 17.8 %all-to-all-start.6 = ((bf16[32,2,3584]{2,1,0:T(2,128)(2,1)}), bf16[32,2,3584]{2,1,0:T(2,128)(2,1)S(1)}, u32[]{:S(2)}, u32[]{:S(2)}) async-start(bf16[32,2,3584]{2,1,0:T(2,128)(2,1)} %reshape.150), calls=%async_computation.6 | async-start | bytes 917504 | tf_op jit(solution)/shard_map/all_to_all | solution.py:94
  243.7 26.5 %all-to-all-start.4 = ((f32[32,1,7168]{2,1,0:T(1,128)}), f32[32,1,7168]{2,1,0:T(1,128)S(1)}, u32[]{:S(2)}, u32[]{:S(2)}) async-start(f32[32,1,7168]{2,1,0:T(1,128)} %copy.36), calls=%async_computation.4 | async-start | bytes 1835008 | tf_op jit(solution)/shard_map/all_to_all | solution.py:92
Sparse Core Ops, SparseCore 0:
  10.1 61.1 all-gather.2
where the time goes:
time: 282 us; the launch traced here: 280 us
  waiting for transfers between devices  94.3 us (33%)
  blocking collectives  66.9 us (24%)
  starting transfers between devices  43.4 us (15%)
  local copies, waits for them, and re-layouts  28.2 us (10%)
  other arithmetic  28.2 us (10%)
  between operations  14.3 us (5%)
  matrix products  4.97 us (2%)
    all_to_all x1, blocking collectives, local(): lax.all_to_all(masked.reshape(groups, row_count, slot_count * tok_slot),...  41 us
    all_to_all x1, blocking collectives, local(): lax.all_to_all(replica_grad.astype(jnp.bfloat16), 'ep', split_axis=0, con...  25.9 us
    all_to_all x1, waiting for transfers between devices, local(): lax.all_to_all(weights, 'ep', split_axis=0, concat_axis=0, tiled=True)  19.8 us
    all_gather x1, waiting for transfers between devices, local(): arrived = lax.all_gather(token_acts[0], 'edp', axis=0, tiled=True)  18 us
    all_to_all x1, waiting for transfers between devices, local(): lax.all_to_all(second_old, 'ep', split_axis=0, concat_axis=0, tiled=True)  12.1 us
    all_to_all x1, waiting for transfers between devices, local(): lax.all_to_all(placed_steps, 'ep', split_axis=0, concat_axis=0, tiled=True)  12.1 us
    all_to_all x1, waiting for transfers between devices, local(): lax.all_to_all(placed_second, 'ep', split_axis=0, concat_axis=0, tiled=True)  11.1 us
    all_to_all x1, waiting for transfers between devices, local(): lax.all_to_all(first_old, 'ep', split_axis=0, concat_axis=0, tiled=True)  10.7 us
  transfers between devices with their start and end apart: 8, of which 7 were waited for; matrix products, arithmetic and copies ran while one was open for 14% of the time, Pallas kernels for 0%

commit v1 on v0

--- a/solution.py
+++ b/solution.py
@@ -1,3 +1,4 @@
+import functools
 import jax
 import jax.numpy as jnp
 from jax import lax
@@ -9,6 +10,38 @@
 bias_two = 0.994079470779666
 decay_rate = 0.1
 adam_eps = 1e-08
+
+
+def _prepare_task(packet, dim_at):
+    packet = jnp.moveaxis(packet, 0, dim_at)
+    small = packet.shape
+    return packet.reshape(*small[:dim_at], small[dim_at] * small[dim_at + 1], *small[dim_at + 2 :])
+
+
+def obtain_node(buf, row_dim, mesh_dim):
+    axis_n = lax.axis_size(mesh_dim)
+    bank = []
+    for nth in range(axis_n):
+        bank.append((nth, (nth + 1) % axis_n))
+    leaves = []
+    for w, ii in bank:
+        leaves.append((ii, w))
+    everything, z = ([], [])
+    for q in range(axis_n - 1):
+        if q % 2 == 0:
+            local_next = lax.ppermute(everything[-1] if everything else buf, mesh_dim, bank)
+            everything.append(local_next)
+        else:
+            later = lax.ppermute(z[-1] if z else buf, mesh_dim, leaves)
+            z.append(later)
+    o_now = jnp.stack([*everything[::-1], buf, *z])
+    main = lax.axis_index(mesh_dim)
+    x_new = main - len(everything)
+    o_now = o_now[(jnp.arange(axis_n) - x_new) % axis_n]
+    return _prepare_task(o_now, row_dim)
+
+
+draw_blocks_on_mesh = functools.partial(obtain_node, row_dim=0, mesh_dim="edp")
 
 
 def adam_update(weights, first_old, second_old, gradient):
@@ -52,7 +85,7 @@
         concat_axis=0,
         tiled=True,
     )
-    arrived = lax.all_gather(token_acts[0], "edp", axis=0, tiled=True)
+    arrived = draw_blocks_on_mesh(token_acts[0])
     count_here = arrived.shape[0]
     grad_block = received
     grad_block = grad_block.reshape(count_here, row_count, slot_count, tok_slot)

time: 282 us -> 313 us (1.11)
  the two profiles are of different devices: /device:TPU:2 before, /device:TPU:192 now
where the time goes in v1:
time: 313 us; the launch traced here: 311 us
  waiting for transfers between devices  126 us (40%)
  starting transfers between devices  73.6 us (24%)
  local copies, waits for them, and re-layouts  53.4 us (17%)
  other arithmetic  29 us (9%)
  blocking collectives  23.2 us (7%)
  matrix products  4.97 us (2%)
    ppermute x7, waiting for transfers between devices, obtain_node(): later = lax.ppermute(z[-1] if z else buf, mesh_dim, leaves)  31.4 us
    unnamed x51, local copies, waits for them, and re-layouts  27.4 us
    all_to_all x1, blocking collectives, local(): lax.all_to_all(replica_grad.astype(jnp.bfloat16), 'ep', split_axis=0, con...  23.2 us
    all_to_all x1, waiting for transfers between devices, local(): lax.all_to_all(weights, 'ep', split_axis=0, concat_axis=0, tiled=True)  21.8 us
    ppermute x8, starting transfers between devices, obtain_node(): lax.ppermute(everything[-1] if everything else buf, mesh_dim, bank)  15.6 us
    all_to_all x1, waiting for transfers between devices, local(): lax.all_to_all(placed_first, 'ep', split_axis=0, concat_axis=0, tiled=True)  15.1 us
    all_to_all x1, waiting for transfers between devices, local(): lax.all_to_all(placed_steps, 'ep', split_axis=0, concat_axis=0, tiled=True)  15 us
    all_to_all x1, waiting for transfers between devices, local(): lax.all_to_all(second_old, 'ep', split_axis=0, concat_axis=0, tiled=True)  14.1 us
  transfers between devices with their start and end apart: 23, of which 13 were waited for; matrix products, arithmetic and copies ran while one was open for 19% of the time, Pallas kernels for 0%

profile of v1, /device:TPU:192, one launch (start us, length us, event | category | flops | bytes accessed | tf_op | source)
XLA Modules:
  0.0 311.5 jit_solution(5077016182521271707)
XLA Ops:
  0.7 1.3 fusion.30
  2.0 1.3 fusion.25
  3.3 3.4 %collective-permute-done = bf16[1,2,64,1024]{3,2,1,0:T(8,128)(2,1)S(1)} collective-permute-done((bf16[1,2,64,1024]{3,2,1,0:T(8,128)(2,1)}, bf16[1,2,64,1024]{3,2,1,0:T(8,128)(2,1)S(1)}, u32[]{:S(2)}, u32[]{:S(2)}) %collective-permute-start) | collective-permute-done | bytes 262176 | tf_op jit(solution)/shard_map/ppermute | solution.py:32
  6.7 1.3 collective-permute-start.1
  8.0 2.2 broadcast_select_fusion
  10.1 8.4 %all-to-all-start = ((bf16[16,224,128]{2,1,0:T(8,128)(2,1)}), bf16[16,224,128]{2,1,0:T(8,128)(2,1)S(1)}, u32[]{:S(2)}, u32[]{:S(2)}) async-start(bf16[16,224,128]{2,1,0:T(8,128)(2,1)} %broadcast_select_fusion), calls=%async_computation | async-start | bytes 1835008 | tf_op jit(solution)/shard_map/all_to_all | solution.py:81
  19.1 23.0 %collective-permute-done.8 = bf16[1,2,64,1024]{3,2,1,0:T(8,128)(2,1)S(1)} collective-permute-done((bf16[1,2,64,1024]{3,2,1,0:T(8,128)(2,1)}, bf16[1,2,64,1024]{3,2,1,0:T(8,128)(2,1)S(1)}, u32[]{:S(2)}, u32[]{:S(2)}) %collective-permute-start.8) | collective-permute-done | bytes 262176 | tf_op jit(solution)/shard_map/ppermute | solution.py:35
  42.0 1.8 collective-permute-start.9
  44.8 3.0 collective-permute-done.9
  47.7 2.1 collective-permute-start.10
  49.9 1.9 collective-permute-start.4
  51.8 2.0 collective-permute-done.10
  53.8 2.2 collective-permute-start.11
  56.0 2.8 collective-permute-start.5
  59.9 2.2 collective-permute-start.12
  62.1 3.7 %collective-permute-start.6 = (bf16[1,2,64,1024]{3,2,1,0:T(8,128)(2,1)S(1)}, bf16[1,2,64,1024]{3,2,1,0:T(8,128)(2,1)}, u32[]{:S(2)}, u32[]{:S(2)}) collective-permute-start(bf16[1,2,64,1024]{3,2,1,0:T(8,128)(2,1)S(1)} %collective-permute-done.5), channel_id=1, source_target_pairs={{0,32},{32,64},{64,96},{96,128},{128,160},{160,192},{192,224},{224... | collective-permute-start | bytes 786440 | tf_op jit(solution)/shard_map/ppermute | solution.py:32
  65.8 1.1 collective-permute-done.12
  66.9 1.3 collective-permute-start.13
  68.2 4.7 %collective-permute-start.7 = (bf16[1,2,64,1024]{3,2,1,0:T(8,128)(2,1)}, bf16[1,2,64,1024]{3,2,1,0:T(8,128)(2,1)}, u32[]{:S(2)}, u32[]{:S(2)}) collective-permute-start(bf16[1,2,64,1024]{3,2,1,0:T(8,128)(2,1)} %collective-permute-done.6), channel_id=1, source_target_pairs={{0,32},{32,64},{64,96},{96,128},{128,160},{160,192},{192,224},{224... | collective-permute-start | bytes 786440 | tf_op jit(solution)/shard_map/ppermute | solution.py:32
  72.9 1.3 collective-permute-done.13
  74.9 1.7 bitcast_dynamic-update-slice_fusion.14
  76.6 1.7 bitcast_dynamic-update-slice_fusion.13
  78.3 1.7 bitcast_dynamic-update-slice_fusion.12
  80.0 1.7 bitcast_dynamic-update-slice_fusion.11
  81.6 1.7 bitcast_dynamic-update-slice_fusion.10
  83.3 1.7 bitcast_dynamic-update-slice_fusion.9
  90.1 1.7 bitcast_dynamic-update-slice_fusion.2
  91.7 1.7 bitcast_dynamic-update-slice_fusion.1
  93.4 1.7 bitcast_dynamic-update-slice_fusion
  95.1 5.0 %gather_fusion = bf16[16,2,64,1024]{3,2,1,0:T(8,128)(2,1)} fusion(bf16[16,2,64,1024]{3,2,1,0:T(8,128)(2,1)} %bitcast.20, s32[1024]{0:T(1024)S(1)} %pad_clamp_fusion), kind=kCustom, calls=%fused_computation | custom fusion | bytes 8388672 | tf_op jit(solution)/shard_map/gather | solution.py:40
  100.1 3.3 %convolution_bitcast_fusion.1 = f32[2,224,1024]{2,1,0:T(8,128)S(1)} fusion(bf16[16,224,2,64]{1,3,2,0:T(8,128)(2,1)S(1)} %bitcast.62, bf16[16,2,64,1024]{3,2,1,0:T(8,128)(2,1)} %gather_fusion), kind=kOutput, calls=%fused_computation.8 | convolution fusion | flops 939524096 | bytes 6946816 | tf_op jit(solution)/shard_map/adst,astf->sdf/dot_general | solution.py:92
  104.4 3.3 %reduce.3 = bf16[32,7168]{1,0:T(8,128)(2,1)S(1)} reduce(bf16[32,1,7168]{2,1,0:T(2,128)(2,1)S(1)} %convert_element_type.77, bf16[]{:T(256)} %broadcast.194), dimensions={1}, to_apply=%convert_element_type.77.reduce_sub_computation | reduce | bytes 917506 | tf_op jit(solution)/shard_map/convert_element_type | solution.py:103
  108.0 23.2 %all_to_all.77 = bf16[32,2,3584]{2,1,0:T(2,128)(2,1)S(1)} all-to-all(bf16[32,2,3584]{2,1,0:T(2,128)(2,1)S(1)} %reshape.207), channel_id=1, replica_groups=mesh['edp'=16,'ep'=32] {'ep'}, dimensions={0} | all-to-all | bytes 917504 | tf_op jit(solution)/shard_map/all_to_all | solution.py:102
  132.8 1.1 reshape.209
  133.8 4.3 %all-to-all-start.2 = ((bf16[32,2,3584]{2,1,0:T(2,128)(2,1)}), bf16[32,2,3584]{2,1,0:T(2,128)(2,1)S(1)}, u32[]{:S(2)}, u32[]{:S(2)}) async-start(bf16[32,2,3584]{2,1,0:T(2,128)(2,1)} %reshape.209), calls=%async_computation.2 | async-start | bytes 917504 | tf_op jit(solution)/shard_map/all_to_all | solution.py:106
  138.2 2.1 convert_multiply_fusion.1
  140.2 1.6 mul.67
  141.8 2.1 convert_multiply_fusion
  143.9 2.5 mul.71
  146.4 2.2 broadcast_multiply_fusion
  148.6 2.6 mul.76
  152.2 1.6 reshape_squeeze.2
  153.8 1.1 reshape.210
  154.9 3.1 %fusion.29 = (bf16[32,1,7168]{2,0,1:T(8,128)(2,1)S(1)}, f32[32,1,7168]{2,0,1:T(8,128)S(1)}, bf16[32,1,7168]{2,0,1:T(8,128)(2,1)}) fusion(f32[32,1,7168]{2,0,1:T(8,128)} %mul.71, f32[32,1,7168]{2,0,1:T(8,128)S(1)} %reshape_squeeze.2, bf16[32,1,7168]{2,1,0:T(2,128)(2,1)} %reshape.210, f32[32,1,7168]{2,0,1:T(8,128)} %mul.76, f32[32,1,7168]{2,0,1:T(8,128)S(1)} %mul.67), kind=kLoop, calls=%fused_computation.69 | loop fusion | flops 3440640 | bytes 5963776 | tf_op jit(solution)/shard_map/convert_element_type | solution.py:52
  158.1 1.8 reduce.5
  161.0 9.6 %all-to-all-start.5 = ((bf16[32,2,3584]{2,1,0:T(2,128)(2,1)}), bf16[32,2,3584]{2,1,0:T(2,128)(2,1)S(1)}, u32[]{:S(2)}, u32[]{:S(2)}) async-start(bf16[32,2,3584]{2,1,0:T(2,128)(2,1)} %reshape.211), calls=%async_computation.5 | async-start | bytes 917504 | tf_op jit(solution)/shard_map/all_to_all | solution.py:114
  172.6 12.4 %all-to-all-done.5 = bf16[32,2,3584]{2,1,0:T(2,128)(2,1)S(1)} async-done(((bf16[32,2,3584]{2,1,0:T(2,128)(2,1)}), bf16[32,2,3584]{2,1,0:T(2,128)(2,1)S(1)}, u32[]{:S(2)}, u32[]{:S(2)}) %all-to-all-start.5) | async-done | bytes 458784 | tf_op jit(solution)/shard_map/all_to_all | solution.py:114
  184.9 6.1 %all-to-all-start.7 = ((bf16[32,2,3584]{2,1,0:T(2,128)(2,1)}), bf16[32,2,3584]{2,1,0:T(2,128)(2,1)S(1)}, u32[]{:S(2)}, u32[]{:S(2)}) async-start(bf16[32,2,3584]{2,1,0:T(2,128)(2,1)} %reshape.215), calls=%async_computation.7 | async-start | bytes 917504 | tf_op jit(solution)/shard_map/all_to_all | solution.py:115
  193.7 14.1 %all-to-all-done.7 = bf16[32,2,3584]{2,1,0:T(2,128)(2,1)S(1)} async-done(((bf16[32,2,3584]{2,1,0:T(2,128)(2,1)}), bf16[32,2,3584]{2,1,0:T(2,128)(2,1)S(1)}, u32[]{:S(2)}, u32[]{:S(2)}) %all-to-all-start.7) | async-done | bytes 458784 | tf_op jit(solution)/shard_map/all_to_all | solution.py:115
  207.8 5.2 %all-to-all-start.6 = ((bf16[32,2,3584]{2,1,0:T(2,128)(2,1)}), bf16[32,2,3584]{2,1,0:T(2,128)(2,1)S(1)}, u32[]{:S(2)}, u32[]{:S(2)}) async-start(bf16[32,2,3584]{2,1,0:T(2,128)(2,1)} %reshape.213), calls=%async_computation.6 | async-start | bytes 917504 | tf_op jit(solution)/shard_map/all_to_all | solution.py:127
  213.0 1.9 copy.34
  214.9 15.1 %all-to-all-done.6 = bf16[32,2,3584]{2,1,0:T(2,128)(2,1)S(1)} async-done(((bf16[32,2,3584]{2,1,0:T(2,128)(2,1)}), bf16[32,2,3584]{2,1,0:T(2,128)(2,1)S(1)}, u32[]{:S(2)}, u32[]{:S(2)}) %all-to-all-start.6) | async-done | bytes 458784 | tf_op jit(solution)/shard_map/all_to_all | solution.py:127
  230.0 4.4 %all-to-all-start.3 = ((f32[32,1,7168]{2,1,0:T(1,128)}), f32[32,1,7168]{2,1,0:T(1,128)S(1)}, u32[]{:S(2)}, u32[]{:S(2)}) async-start(f32[32,1,7168]{2,1,0:T(1,128)} %copy.34), calls=%async_computation.3 | async-start | bytes 1835008 | tf_op jit(solution)/shard_map/all_to_all | solution.py:112
  237.1 21.8 %all-to-all-done.3 = f32[32,1,7168]{2,1,0:T(1,128)S(1)} async-done(((f32[32,1,7168]{2,1,0:T(1,128)}), f32[32,1,7168]{2,1,0:T(1,128)S(1)}, u32[]{:S(2)}, u32[]{:S(2)}) %all-to-all-start.3) | async-done | bytes 917536 | tf_op jit(solution)/shard_map/all_to_all | solution.py:112
  258.9 5.5 %all-to-all-start.8 = ((bf16[32,2,3584]{2,1,0:T(2,128)(2,1)}), bf16[32,2,3584]{2,1,0:T(2,128)(2,1)S(1)}, u32[]{:S(2)}, u32[]{:S(2)}) async-start(bf16[32,2,3584]{2,1,0:T(2,128)(2,1)} %reshape.217), calls=%async_computation.8 | async-start | bytes 917504 | tf_op jit(solution)/shard_map/all_to_all | solution.py:128
  265.1 1.9 copy.35
  267.0 13.0 %all-to-all-done.8 = bf16[32,2,3584]{2,1,0:T(2,128)(2,1)S(1)} async-done(((bf16[32,2,3584]{2,1,0:T(2,128)(2,1)}), bf16[32,2,3584]{2,1,0:T(2,128)(2,1)S(1)}, u32[]{:S(2)}, u32[]{:S(2)}) %all-to-all-start.8) | async-done | bytes 458784 | tf_op jit(solution)/shard_map/all_to_all | solution.py:128
  280.0 4.4 %all-to-all-start.4 = ((f32[32,1,7168]{2,1,0:T(1,128)}), f32[32,1,7168]{2,1,0:T(1,128)S(1)}, u32[]{:S(2)}, u32[]{:S(2)}) async-start(f32[32,1,7168]{2,1,0:T(1,128)} %copy.35), calls=%async_computation.4 | async-start | bytes 1835008 | tf_op jit(solution)/shard_map/all_to_all | solution.py:125
  284.8 2.7 reduce.1
  287.6 1.3 reshape.190
  289.2 2.7 reduce.2
  292.0 1.3 reshape.191
  293.2 15.0 %all-to-all-done.4 = f32[32,1,7168]{2,1,0:T(1,128)S(1)} async-done(((f32[32,1,7168]{2,1,0:T(1,128)}), f32[32,1,7168]{2,1,0:T(1,128)S(1)}, u32[]{:S(2)}, u32[]{:S(2)}) %all-to-all-start.4) | async-done | bytes 917536 | tf_op jit(solution)/shard_map/all_to_all | solution.py:125
  308.2 2.2 reduce
  (73 shorter events, 22.8 us)
Async XLA Ops:
  0.6 6.0 %collective-permute-start = (bf16[1,2,64,1024]{3,2,1,0:T(8,128)(2,1)}, bf16[1,2,64,1024]{3,2,1,0:T(8,128)(2,1)S(1)}, u32[]{:S(2)}, u32[]{:S(2)}) collective-permute-start(bf16[1,2,64,1024]{3,2,1,0:T(8,128)(2,1)} %bitcast.64), channel_id=1, source_target_pairs={{0,32},{32,64},{64,96},{96,128},{128,160},{160,192},{192,224},{224... | collective-permute-start | bytes 786440 | tf_op jit(solution)/shard_map/ppermute | solution.py:32
  6.7 12.2 %collective-permute-start.1 = (bf16[1,2,64,1024]{3,2,1,0:T(8,128)(2,1)S(1)}, bf16[1,2,64,1024]{3,2,1,0:T(8,128)(2,1)S(1)}, u32[]{:S(2)}, u32[]{:S(2)}) collective-permute-start(bf16[1,2,64,1024]{3,2,1,0:T(8,128)(2,1)S(1)} %collective-permute-done), channel_id=1, source_target_pairs={{0,32},{32,64},{64,96},{96,128},{128,160},{160,192},{192,224},{224... | collective-permute-start | bytes 786440 | tf_op jit(solution)/shard_map/ppermute | solution.py:32
  10.1 76.3 %copy-start = (bf16[1,1,2,64,1024]{4,3,2,1,0:T(8,128)(2,1)S(1)}, bf16[1,1,2,64,1024]{4,3,2,1,0:T(8,128)(2,1)}, u32[]{:S(2)}) copy-start(bf16[1,1,2,64,1024]{4,3,2,1,0:T(8,128)(2,1)} %param.9) | copy-start | bytes 786436
  10.1 64.2 %all-to-all-start = ((bf16[16,224,128]{2,1,0:T(8,128)(2,1)}), bf16[16,224,128]{2,1,0:T(8,128)(2,1)S(1)}, u32[]{:S(2)}, u32[]{:S(2)}) async-start(bf16[16,224,128]{2,1,0:T(8,128)(2,1)} %broadcast_select_fusion), calls=%async_computation | async-start | bytes 1835008 | tf_op jit(solution)/shard_map/all_to_all | solution.py:81
  18.6 23.5 %collective-permute-start.8 = (bf16[1,2,64,1024]{3,2,1,0:T(8,128)(2,1)}, bf16[1,2,64,1024]{3,2,1,0:T(8,128)(2,1)S(1)}, u32[]{:S(2)}, u32[]{:S(2)}) collective-permute-start(bf16[1,2,64,1024]{3,2,1,0:T(8,128)(2,1)} %bitcast.65), channel_id=1, source_target_pairs={{32,0},{64,32},{96,64},{128,96},{160,128},{192,160},{224,192},{256... | collective-permute-start | bytes 786440 | tf_op jit(solution)/shard_map/ppermute | solution.py:35
  18.9 25.0 %collective-permute-start.2 = (bf16[1,2,64,1024]{3,2,1,0:T(8,128)(2,1)S(1)}, bf16[1,2,64,1024]{3,2,1,0:T(8,128)(2,1)S(1)}, u32[]{:S(2)}, u32[]{:S(2)}) collective-permute-start(bf16[1,2,64,1024]{3,2,1,0:T(8,128)(2,1)S(1)} %collective-permute-done.1), channel_id=1, source_target_pairs={{0,32},{32,64},{64,96},{96,128},{128,160},{160,192},{192,224},{224... | collective-permute-start | bytes 786440 | tf_op jit(solution)/shard_map/ppermute | solution.py:32
  42.0 5.7 %collective-permute-start.9 = (bf16[1,2,64,1024]{3,2,1,0:T(8,128)(2,1)S(1)}, bf16[1,2,64,1024]{3,2,1,0:T(8,128)(2,1)S(1)}, u32[]{:S(2)}, u32[]{:S(2)}) collective-permute-start(bf16[1,2,64,1024]{3,2,1,0:T(8,128)(2,1)S(1)} %collective-permute-done.8), channel_id=1, source_target_pairs={{32,0},{64,32},{96,64},{128,96},{160,128},{192,160},{224,192},{256... | collective-permute-start | bytes 786440 | tf_op jit(solution)/shard_map/ppermute | solution.py:35
  43.9 30.5 %copy-start.1 = (bf16[1,2,64,1024]{3,2,1,0:T(8,128)(2,1)}, bf16[1,2,64,1024]{3,2,1,0:T(8,128)(2,1)S(1)}, u32[]{:S(2)}) copy-start(bf16[1,2,64,1024]{3,2,1,0:T(8,128)(2,1)S(1)} %collective-permute-done.2) | copy-start | bytes 786436
  43.9 6.0 %collective-permute-start.3 = (bf16[1,2,64,1024]{3,2,1,0:T(8,128)(2,1)S(1)}, bf16[1,2,64,1024]{3,2,1,0:T(8,128)(2,1)S(1)}, u32[]{:S(2)}, u32[]{:S(2)}) collective-permute-start(bf16[1,2,64,1024]{3,2,1,0:T(8,128)(2,1)S(1)} %collective-permute-done.2), channel_id=1, source_target_pairs={{0,32},{32,64},{64,96},{96,128},{128,160},{160,192},{192,224},{224... | collective-permute-start | bytes 786440 | tf_op jit(solution)/shard_map/ppermute | solution.py:32
  47.7 6.0 %collective-permute-start.10 = (bf16[1,2,64,1024]{3,2,1,0:T(8,128)(2,1)S(1)}, bf16[1,2,64,1024]{3,2,1,0:T(8,128)(2,1)S(1)}, u32[]{:S(2)}, u32[]{:S(2)}) collective-permute-start(bf16[1,2,64,1024]{3,2,1,0:T(8,128)(2,1)S(1)} %collective-permute-done.9), channel_id=1, source_target_pairs={{32,0},{64,32},{96,64},{128,96},{160,128},{192,160},{224,192},{256... | collective-permute-start | bytes 786440 | tf_op jit(solution)/shard_map/ppermute | solution.py:35
  49.9 24.5 %copy-start.6 = (bf16[1,2,64,1024]{3,2,1,0:T(8,128)(2,1)}, bf16[1,2,64,1024]{3,2,1,0:T(8,128)(2,1)S(1)}, u32[]{:S(2)}) copy-start(bf16[1,2,64,1024]{3,2,1,0:T(8,128)(2,1)S(1)} %collective-permute-done.3) | copy-start | bytes 786436
  49.9 6.1 %collective-permute-start.4 = (bf16[1,2,64,1024]{3,2,1,0:T(8,128)(2,1)S(1)}, bf16[1,2,64,1024]{3,2,1,0:T(8,128)(2,1)S(1)}, u32[]{:S(2)}, u32[]{:S(2)}) collective-permute-start(bf16[1,2,64,1024]{3,2,1,0:T(8,128)(2,1)S(1)} %collective-permute-done.3), channel_id=1, source_target_pairs={{0,32},{32,64},{64,96},{96,128},{128,160},{160,192},{192,224},{224... | collective-permute-start | bytes 786440 | tf_op jit(solution)/shard_map/ppermute | solution.py:32
  53.8 20.6 %copy-start.2 = (bf16[1,2,64,1024]{3,2,1,0:T(8,128)(2,1)}, bf16[1,2,64,1024]{3,2,1,0:T(8,128)(2,1)S(1)}, u32[]{:S(2)}) copy-start(bf16[1,2,64,1024]{3,2,1,0:T(8,128)(2,1)S(1)} %collective-permute-done.10) | copy-start | bytes 786436
  53.8 6.1 %collective-permute-start.11 = (bf16[1,2,64,1024]{3,2,1,0:T(8,128)(2,1)S(1)}, bf16[1,2,64,1024]{3,2,1,0:T(8,128)(2,1)S(1)}, u32[]{:S(2)}, u32[]{:S(2)}) collective-permute-start(bf16[1,2,64,1024]{3,2,1,0:T(8,128)(2,1)S(1)} %collective-permute-done.10), channel_id=1, source_target_pairs={{32,0},{64,32},{96,64},{128,96},{160,128},{192,160},{224,192},{256... | collective-permute-start | bytes 786440 | tf_op jit(solution)/shard_map/ppermute | solution.py:35
  56.0 11.0 %copy-start.7 = (bf16[1,2,64,1024]{3,2,1,0:T(8,128)(2,1)}, bf16[1,2,64,1024]{3,2,1,0:T(8,128)(2,1)S(1)}, u32[]{:S(2)}) copy-start(bf16[1,2,64,1024]{3,2,1,0:T(8,128)(2,1)S(1)} %collective-permute-done.4) | copy-start | bytes 786436
  56.0 6.1 %collective-permute-start.5 = (bf16[1,2,64,1024]{3,2,1,0:T(8,128)(2,1)S(1)}, bf16[1,2,64,1024]{3,2,1,0:T(8,128)(2,1)S(1)}, u32[]{:S(2)}, u32[]{:S(2)}) collective-permute-start(bf16[1,2,64,1024]{3,2,1,0:T(8,128)(2,1)S(1)} %collective-permute-done.4), channel_id=1, source_target_pairs={{0,32},{32,64},{64,96},{96,128},{128,160},{160,192},{192,224},{224... | collective-permute-start | bytes 786440 | tf_op jit(solution)/shard_map/ppermute | solution.py:32
  59.9 14.5 %copy-start.4 = (bf16[1,2,64,1024]{3,2,1,0:T(8,128)(2,1)}, bf16[1,2,64,1024]{3,2,1,0:T(8,128)(2,1)S(1)}, u32[]{:S(2)}) copy-start(bf16[1,2,64,1024]{3,2,1,0:T(8,128)(2,1)S(1)} %collective-permute-done.11) | copy-start | bytes 786436
  59.9 7.1 %collective-permute-start.12 = (bf16[1,2,64,1024]{3,2,1,0:T(8,128)(2,1)S(1)}, bf16[1,2,64,1024]{3,2,1,0:T(8,128)(2,1)}, u32[]{:S(2)}, u32[]{:S(2)}) collective-permute-start(bf16[1,2,64,1024]{3,2,1,0:T(8,128)(2,1)S(1)} %collective-permute-done.11), channel_id=1, source_target_pairs={{32,0},{64,32},{96,64},{128,96},{160,128},{192,160},{224,192},{256... | collective-permute-start | bytes 786440 | tf_op jit(solution)/shard_map/ppermute | solution.py:35
  62.1 6.1 %copy-start.8 = (bf16[1,2,64,1024]{3,2,1,0:T(8,128)(2,1)}, bf16[1,2,64,1024]{3,2,1,0:T(8,128)(2,1)S(1)}, u32[]{:S(2)}) copy-start(bf16[1,2,64,1024]{3,2,1,0:T(8,128)(2,1)S(1)} %collective-permute-done.5) | copy-start | bytes 786436
  62.1 6.1 %collective-permute-start.6 = (bf16[1,2,64,1024]{3,2,1,0:T(8,128)(2,1)S(1)}, bf16[1,2,64,1024]{3,2,1,0:T(8,128)(2,1)}, u32[]{:S(2)}, u32[]{:S(2)}) collective-permute-start(bf16[1,2,64,1024]{3,2,1,0:T(8,128)(2,1)S(1)} %collective-permute-done.5), channel_id=1, source_target_pairs={{0,32},{32,64},{64,96},{96,128},{128,160},{160,192},{192,224},{224... | collective-permute-start | bytes 786440 | tf_op jit(solution)/shard_map/ppermute | solution.py:32
  66.9 7.3 %collective-permute-start.13 = (bf16[1,2,64,1024]{3,2,1,0:T(8,128)(2,1)}, bf16[1,2,64,1024]{3,2,1,0:T(8,128)(2,1)}, u32[]{:S(2)}, u32[]{:S(2)}) collective-permute-start(bf16[1,2,64,1024]{3,2,1,0:T(8,128)(2,1)} %collective-permute-done.12), channel_id=1, source_target_pairs={{32,0},{64,32},{96,64},{128,96},{160,128},{192,160},{224,192},{256... | collective-permute-start | bytes 786440 | tf_op jit(solution)/shard_map/ppermute | solution.py:35
  68.2 6.7 %collective-permute-start.7 = (bf16[1,2,64,1024]{3,2,1,0:T(8,128)(2,1)}, bf16[1,2,64,1024]{3,2,1,0:T(8,128)(2,1)}, u32[]{:S(2)}, u32[]{:S(2)}) collective-permute-start(bf16[1,2,64,1024]{3,2,1,0:T(8,128)(2,1)} %collective-permute-done.6), channel_id=1, source_target_pairs={{0,32},{32,64},{64,96},{96,128},{128,160},{160,192},{192,224},{224... | collective-permute-start | bytes 786440 | tf_op jit(solution)/shard_map/ppermute | solution.py:32
  74.3 19.2 %collective-permute-start.14 = (bf16[1,2,64,1024]{3,2,1,0:T(8,128)(2,1)}, bf16[1,2,64,1024]{3,2,1,0:T(8,128)(2,1)}, u32[]{:S(2)}, u32[]{:S(2)}) collective-permute-start(bf16[1,2,64,1024]{3,2,1,0:T(8,128)(2,1)} %collective-permute-done.13), channel_id=1, source_target_pairs={{32,0},{64,32},{96,64},{128,96},{160,128},{192,160},{224,192},{256... | collective-permute-start | bytes 786440 | tf_op jit(solution)/shard_map/ppermute | solution.py:35
  74.9 13.7 %copy-start.3 = (bf16[1,2,64,1024]{3,2,1,0:T(8,128)(2,1)S(1)}, bf16[1,2,64,1024]{3,2,1,0:T(8,128)(2,1)}, u32[]{:S(2)}) copy-start(bf16[1,2,64,1024]{3,2,1,0:T(8,128)(2,1)} %copy-done.2) | copy-start | bytes 786436
  74.9 14.5 %copy-start.5 = (bf16[1,2,64,1024]{3,2,1,0:T(8,128)(2,1)S(1)}, bf16[1,2,64,1024]{3,2,1,0:T(8,128)(2,1)}, u32[]{:S(2)}) copy-start(bf16[1,2,64,1024]{3,2,1,0:T(8,128)(2,1)} %copy-done.4) | copy-start | bytes 786436
  103.4 28.2 %copy-start.9 = (s32[32]{0:T(128)S(1)}, s32[32]{0:T(128)}, u32[]{:S(2)}) copy-start(s32[32]{0:T(128)} %param.15) | copy-start | bytes 388
  103.4 28.2 %copy-start.11 = (s32[32]{0:T(128)S(1)}, s32[32]{0:T(128)}, u32[]{:S(2)}) copy-start(s32[32]{0:T(128)} %param.16) | copy-start | bytes 388
  133.8 19.9 %all-to-all-start.2 = ((bf16[32,2,3584]{2,1,0:T(2,128)(2,1)}), bf16[32,2,3584]{2,1,0:T(2,128)(2,1)S(1)}, u32[]{:S(2)}, u32[]{:S(2)}) async-start(bf16[32,2,3584]{2,1,0:T(2,128)(2,1)} %reshape.209), calls=%async_computation.2 | async-start | bytes 917504 | tf_op jit(solution)/shard_map/all_to_all | solution.py:106
  158.1 33.4 %copy-start.10 = (s32[32]{0:T(128)S(1)}, s32[32]{0:T(128)}, u32[]{:S(2)}) copy-start(s32[32]{0:T(128)} %param.17) | copy-start | bytes 388
  161.0 23.9 %all-to-all-start.5 = ((bf16[32,2,3584]{2,1,0:T(2,128)(2,1)}), bf16[32,2,3584]{2,1,0:T(2,128)(2,1)S(1)}, u32[]{:S(2)}, u32[]{:S(2)}) async-start(bf16[32,2,3584]{2,1,0:T(2,128)(2,1)} %reshape.211), calls=%async_computation.5 | async-start | bytes 917504 | tf_op jit(solution)/shard_map/all_to_all | solution.py:114
  184.9 22.9 %all-to-all-start.7 = ((bf16[32,2,3584]{2,1,0:T(2,128)(2,1)}), bf16[32,2,3584]{2,1,0:T(2,128)(2,1)S(1)}, u32[]{:S(2)}, u32[]{:S(2)}) async-start(bf16[32,2,3584]{2,1,0:T(2,128)(2,1)} %reshape.215), calls=%async_computation.7 | async-start | bytes 917504 | tf_op jit(solution)/shard_map/all_to_all | solution.py:115
  207.8 22.2 %all-to-all-start.6 = ((bf16[32,2,3584]{2,1,0:T(2,128)(2,1)}), bf16[32,2,3584]{2,1,0:T(2,128)(2,1)S(1)}, u32[]{:S(2)}, u32[]{:S(2)}) async-start(bf16[32,2,3584]{2,1,0:T(2,128)(2,1)} %reshape.213), calls=%async_computation.6 | async-start | bytes 917504 | tf_op jit(solution)/shard_map/all_to_all | solution.py:127
  230.0 28.9 %all-to-all-start.3 = ((f32[32,1,7168]{2,1,0:T(1,128)}), f32[32,1,7168]{2,1,0:T(1,128)S(1)}, u32[]{:S(2)}, u32[]{:S(2)}) async-start(f32[32,1,7168]{2,1,0:T(1,128)} %copy.34), calls=%async_computation.3 | async-start | bytes 1835008 | tf_op jit(solution)/shard_map/all_to_all | solution.py:112
  258.9 21.1 %all-to-all-start.8 = ((bf16[32,2,3584]{2,1,0:T(2,128)(2,1)}), bf16[32,2,3584]{2,1,0:T(2,128)(2,1)S(1)}, u32[]{:S(2)}, u32[]{:S(2)}) async-start(bf16[32,2,3584]{2,1,0:T(2,128)(2,1)} %reshape.217), calls=%async_computation.8 | async-start | bytes 917504 | tf_op jit(solution)/shard_map/all_to_all | solution.py:128
  280.0 28.2 %all-to-all-start.4 = ((f32[32,1,7168]{2,1,0:T(1,128)}), f32[32,1,7168]{2,1,0:T(1,128)S(1)}, u32[]{:S(2)}, u32[]{:S(2)}) async-start(f32[32,1,7168]{2,1,0:T(1,128)} %copy.35), calls=%async_computation.4 | async-start | bytes 1835008 | tf_op jit(solution)/shard_map/all_to_all | solution.py:125
